TPU v7x, 256 devices: a whole 4x4x8 slice. The times are simulated.
256 devices in a mesh: star: 8 (over x, core), row: 32 (over z, y).
Axes of the slice: x: 4, y: 4, z: 8, core: 2. Of those that a mesh axis runs over, the one named last changes fastest.
Arguments:
- feature_maps: bfloat16 [64, 1024, 1024], P(None, 'row'), may hold values from -6 to 6
- coef_table: bfloat16 [64, 64], replicated, may hold values from -0.119628906 to 0.119628906
- star_counts: int32 [8], replicated, may hold values from 1 to 12, 32 in all
- star_cells: int32 [8, 12], replicated, may hold values from 0 to 63
- star_bands: int32 [8, 12], replicated, may hold values from 0 to 7
- psf_cotangent: bfloat16 [96, 1024, 1024], P('star', 'row'), may hold values from -6 to 6
Outputs:
- map_grad: float32 [64, 1024, 1024], P('star', 'row')
- coef_grad: float32 [64, 64], replicated
Inputs may be any that keep to these rules, and one draw needn't show every extreme that they name: The live stars of group g fill its slots 0 to star_counts[g] - 1; the counts sum to 32, and some group has exactly 12.
All inputs are finite; a program needn't handle non-finite values.
Results may differ from a plain program's by a relative error of at most 0.008.
Values may be sent and summed in bfloat16 or wider, within the bound.
No kernel may reach another device: no remote copies, remote signals or barrier semaphores. Data moves between devices by JAX's collectives and lax.ppermute only.
A program may use at most 128 MiB of HBM per device.

v0:
```python
import jax
import jax.numpy as jnp
from jax import lax
from jax.sharding import PartitionSpec as P

BANDS = 8


def fourier_tables(pupil_size):
    index_row = jnp.arange(pupil_size, dtype=jnp.int32)
    products = index_row[:, None] * index_row[None, :] % pupil_size
    angles = 2.0 * jnp.pi / pupil_size * products.astype(jnp.float32)
    return (jnp.cos(angles).astype(jnp.bfloat16), (-jnp.sin(angles)).astype(jnp.bfloat16))


def aperture_rows(first_row, row_count, pupil_size):
    centre = 0.5 * (pupil_size - 1)
    row_pos = (first_row + jnp.arange(row_count, dtype=jnp.int32)).astype(jnp.float32) - centre
    col_pos = jnp.arange(pupil_size, dtype=jnp.int32).astype(jnp.float32) - centre
    radius = row_pos[:, None] * row_pos[:, None] + col_pos[None, :] * col_pos[None, :]
    return jnp.where(radius <= 0.25 * pupil_size * pupil_size, 1.0, 0.0).astype(jnp.float32)


def wave_numbers(band_ids):
    wavelength = 0.55 + 0.35 * band_ids.astype(jnp.float32) / (BANDS - 1)
    return 2.0 * jnp.pi / wavelength


def table_pick(values, indices):
    positions = jnp.arange(values.shape[0], dtype=jnp.int32)
    chosen = jnp.where(positions[None, :] == indices[:, None], values[None, :], 0)
    return jnp.sum(chosen, axis=1)


def per_device(feature_maps, coef_table, star_counts, star_cells, star_bands, psf_cotangent):
    groups = lax.axis_size("star")
    my_group = lax.axis_index("star")
    slot_count = psf_cotangent.shape[0]
    map_count, row_count, pupil_size = feature_maps.shape
    flat_cells = star_cells.reshape(-1)
    flat_bands = star_bands.reshape(-1)
    cell_count = coef_table.shape[0]
    within = jnp.arange(slot_count, dtype=jnp.int32)
    owner_group = jnp.zeros_like(within) + my_group
    live_mask = within < table_pick(star_counts, owner_group)
    owner_group, within, live_mask = (owner_group, within, live_mask)
    slot_index = owner_group * slot_count + within
    cell_ids = table_pick(flat_cells, slot_index)
    band_ids = table_pick(flat_bands, slot_index)
    cell_hot = cell_ids[:, None] == jnp.arange(cell_count, dtype=jnp.int32)[None, :]
    coef_rows = jnp.dot(
        cell_hot.astype(jnp.bfloat16), coef_table, preferred_element_type=jnp.float32
    ).astype(jnp.bfloat16)
    flat_maps = feature_maps.reshape(map_count, row_count * pupil_size)
    path_error = jnp.dot(coef_rows, flat_maps, preferred_element_type=jnp.float32).reshape(
        -1, row_count, pupil_size
    )
    wave_number = wave_numbers(band_ids)
    phase_angle = wave_number[:, None, None] * path_error
    aperture = aperture_rows(lax.axis_index("row") * row_count, row_count, pupil_size)
    cos_phase = jnp.cos(phase_angle)
    sin_phase = jnp.sin(phase_angle)
    pupil_field = jnp.stack([aperture * cos_phase, aperture * sin_phase], 1).astype(jnp.bfloat16)
    cos_table, sin_table = fourier_tables(pupil_size)
    inverse = 1.0 / pupil_size
    along_cos = jnp.einsum(
        "sarc,cv->sarv", pupil_field, cos_table, preferred_element_type=jnp.float32
    )
    along_sin = jnp.einsum(
        "sarc,cv->sarv", pupil_field, sin_table, preferred_element_type=jnp.float32
    )
    column_field = jnp.stack(
        [along_cos[:, 0] - along_sin[:, 1], along_sin[:, 0] + along_cos[:, 1]], 1
    ).astype(jnp.bfloat16)
    pieces = lax.all_to_all(column_field, "row", split_axis=3, concat_axis=2, tiled=True)
    row_cos = jnp.einsum("sarv,ru->savu", pieces, cos_table, preferred_element_type=jnp.float32)
    row_sin = jnp.einsum("sarv,ru->savu", pieces, sin_table, preferred_element_type=jnp.float32)
    real_part = (row_cos[:, 0] - row_sin[:, 1]) * inverse
    imag_part = (row_sin[:, 0] + row_cos[:, 1]) * inverse
    focal_field = jnp.stack([real_part, imag_part], 1)
    weight = jnp.where(live_mask, 2.0, 0.0).astype(jnp.float32)[:, None, None, None]
    focal_grad = (weight * psf_cotangent.astype(jnp.float32)[:, None] * focal_field).astype(
        jnp.bfloat16
    )
    back_cos = jnp.einsum(
        "savu,ur->savr", focal_grad, cos_table, preferred_element_type=jnp.float32
    )
    back_sin = jnp.einsum(
        "savu,ur->savr", focal_grad, sin_table, preferred_element_type=jnp.float32
    )
    spectrum_grad = jnp.stack(
        [(back_cos[:, 0] + back_sin[:, 1]) * inverse, (back_cos[:, 1] - back_sin[:, 0]) * inverse],
        1,
    ).astype(jnp.bfloat16)
    pieces = lax.all_to_all(spectrum_grad, "row", split_axis=3, concat_axis=2, tiled=True)
    col_cos = jnp.einsum("savr,vc->sarc", pieces, cos_table, preferred_element_type=jnp.float32)
    col_sin = jnp.einsum("savr,vc->sarc", pieces, sin_table, preferred_element_type=jnp.float32)
    pupil_grad = jnp.stack([col_cos[:, 0] + col_sin[:, 1], col_cos[:, 1] - col_sin[:, 0]], 1)
    phase_grad = aperture * (cos_phase * pupil_grad[:, 1] - sin_phase * pupil_grad[:, 0])
    path_grad = (
        (wave_number[:, None, None] * phase_grad)
        .astype(jnp.bfloat16)
        .reshape(-1, row_count * pupil_size)
    )
    map_scores = lax.dot_general(
        path_grad, flat_maps, (((1,), (1,)), ((), ())), preferred_element_type=jnp.float32
    )
    coef_part = lax.dot_general(
        cell_hot.astype(jnp.float32),
        map_scores * (1.0 / (8 * pupil_size)),
        (((0,), (0,)), ((), ())),
        precision=lax.Precision.HIGHEST,
    )
    coef_grad = lax.psum(coef_part, ("star", "row"))
    share = map_count // groups
    map_grad = lax.psum_scatter(
        lax.dot_general(
            coef_rows, path_grad, (((0,), (0,)), ((), ())), preferred_element_type=jnp.float32
        ),
        "star",
        scatter_dimension=0,
        tiled=True,
    )
    return (map_grad.reshape(share, row_count, pupil_size), coef_grad)


def solution(mesh):
    placed = (P(None, "row", None), P(), P(), P(), P(), P("star", "row", None))
    return jax.shard_map(
        per_device,
        mesh=mesh,
        in_specs=placed,
        out_specs=(P("star", "row", None), P()),
        check_vma=False,
    )
```

profile of v0, /device:TPU:1, one launch (start us, length us, event | category | flops | bytes accessed | tf_op | source)
XLA Modules:
  0.0 501.8 jit_solution(5607141360308045111)
XLA Ops:
  16.0 8.4 %fusion.54 = (bf16[12,1,32,1024]{3,0,2,1:T(8,128)(2,1)S(1)}, bf16[12,1,32,1024]{3,0,2,1:T(8,128)(2,1)S(1)}) fusion(f32[12,32,1024]{2,0,1:T(8,128)S(1)} %fusion.3, f32[32,1024]{1,0:T(8,128)S(1)} %fusion.56, f32[12]{0:T(128)S(1)} %add_divide_fusion), kind=kLoop, calls=%fused_computation.67 | loop fusion | flops 1966080 | bytes 3276848 | tf_op jit(solution)/shard_map/stack | solution.py:63
  24.7 17.9 %fusion.28 = f32[12,2,32,1024]{3,2,1,0:T(8,128)S(1)} fusion(bf16[12,2,32,1024]{3,0,2,1:T(8,128)(2,1)S(1)} %pad_maximum_fusion), kind=kOutput, calls=%fused_computation.36 | convolution fusion | flops 1627389952 | bytes 4718592 | tf_op jit(solution)/shard_map/sarc,cv->sarv/dot_general | solution.py:69
  42.5 17.3 %fusion.36 = f32[12,2,32,1024]{3,2,1,0:T(8,128)S(1)} fusion(bf16[12,2,32,1024]{3,0,2,1:T(8,128)(2,1)S(1)} %pad_maximum_fusion), kind=kOutput, calls=%fused_computation.40 | convolution fusion | flops 1626341376 | bytes 4718592 | tf_op jit(solution)/shard_map/sarc,cv->sarv/dot_general | solution.py:66
  62.4 15.1 %copy.45 = bf16[12,2,32,1024]{2,1,0,3:T(2,128)(2,1)} copy(bf16[12,2,32,1024]{3,2,1,0:T(8,128)(2,1)} %pad_maximum_fusion.1) | data formatting | bytes 3145728 | tf_op jit(solution)/shard_map/stack | solution.py:72
  77.5 13.8 %reshape.93 = bf16[32,2,12288]{2,1,0:T(2,128)(2,1)} reshape(bf16[1024,12,2,32]{3,2,1,0:T(2,128)(2,1)} %bitcast.93) | data formatting | bytes 3145728
  91.3 12.3 %all-to-all-start = ((bf16[32,2,12288]{2,1,0:T(2,128)(2,1)}), bf16[32,2,12288]{2,1,0:T(2,128)(2,1)}, u32[]{:S(2)}, u32[]{:S(2)}) async-start(bf16[32,2,12288]{2,1,0:T(2,128)(2,1)} %reshape.93), calls=%async_computation | async-start | bytes 3145728 | tf_op jit(solution)/shard_map/all_to_all | solution.py:75
  105.2 36.3 %all-to-all-done = bf16[32,2,12288]{2,1,0:T(2,128)(2,1)} async-done(((bf16[32,2,12288]{2,1,0:T(2,128)(2,1)}), bf16[32,2,12288]{2,1,0:T(2,128)(2,1)}, u32[]{:S(2)}, u32[]{:S(2)}) %all-to-all-start) | async-done | bytes 1572896 | tf_op jit(solution)/shard_map/all_to_all | solution.py:75
  141.5 14.3 %reshape.94 = bf16[1024,12,2,32]{3,2,1,0:T(2,128)(2,1)} reshape(bf16[32,2,12288]{2,1,0:T(2,128)(2,1)} %all-to-all-done) | data formatting | bytes 3145728
  155.7 9.5 %copy.107 = bf16[12,2,32,32,32]{2,3,4,1,0:T(8,128)(2,1)} copy(bf16[12,2,32,32,32]{2,1,0,4,3:T(2,128)(2,1)} %bitcast.89) | data formatting | bytes 3145728 | tf_op jit(solution)/shard_map/all_to_all | solution.py:75
  165.2 9.8 %all_to_all.29 = bf16[12,2,1024,32]{2,3,1,0:T(8,128)(2,1)} reshape(bf16[12,2,32,32,32]{3,2,4,1,0:T(8,128)(2,1)} %bitcast.90) | data formatting | bytes 3145728 | tf_op jit(solution)/shard_map/all_to_all | solution.py:75
  175.0 18.3 %fusion.26 = f32[12,2,32,1024]{3,2,1,0:T(8,128)S(1)} fusion(bf16[12,2,1024,32]{2,3,1,0:T(8,128)(2,1)} %all_to_all.29), kind=kOutput, calls=%fused_computation.35 | convolution fusion | flops 1627389952 | bytes 4718592 | tf_op jit(solution)/shard_map/sarv,ru->savu/dot_general | solution.py:77
  193.3 17.4 %fusion.34 = f32[12,2,32,1024]{3,2,1,0:T(8,128)S(1)} fusion(bf16[12,2,1024,32]{2,3,1,0:T(8,128)(2,1)S(1)} %copy-done.3), kind=kOutput, calls=%fused_computation.39 | convolution fusion | flops 1626341376 | bytes 4718592 | tf_op jit(solution)/shard_map/sarv,ru->savu/dot_general | solution.py:76
  212.1 16.4 %fusion.32 = f32[12,2,32,1024]{3,2,1,0:T(8,128)S(1)} fusion(f32[12,1,32,1024]{3,2,1,0:T(8,128)S(1)} %get-tuple-element.15, f32[12,1,32,1024]{3,2,1,0:T(8,128)S(1)} %get-tuple-element.14, f32[12,32,1024]{2,1,0:T(8,128)S(1)} %copy-done.2), kind=kOutput, calls=%fused_computation.38 | convolution fusion | flops 1628700672 | bytes 7864320 | tf_op jit(solution)/shard_map/savu,ur->savr/dot_general | solution.py:85
  228.5 16.7 %fusion.24 = f32[12,2,32,1024]{3,2,1,0:T(8,128)S(1)} fusion(f32[12,1,32,1024]{3,2,1,0:T(8,128)S(1)} %get-tuple-element.15, f32[12,1,32,1024]{3,2,1,0:T(8,128)S(1)} %get-tuple-element.14, f32[12,32,1024]{2,1,0:T(8,128)S(1)} %copy-done.2), kind=kOutput, calls=%fused_computation.34 | convolution fusion | flops 1629749248 | bytes 7864320 | tf_op jit(solution)/shard_map/savu,ur->savr/dot_general | solution.py:88
  247.2 15.1 %copy.47 = bf16[12,2,32,1024]{2,1,0,3:T(2,128)(2,1)} copy(bf16[12,2,32,1024]{3,2,1,0:T(8,128)(2,1)} %pad_maximum_fusion.2) | data formatting | bytes 3145728 | tf_op jit(solution)/shard_map/stack | solution.py:91
  262.3 14.2 %reshape.95 = bf16[32,2,12288]{2,1,0:T(2,128)(2,1)} reshape(bf16[1024,12,2,32]{3,2,1,0:T(2,128)(2,1)} %bitcast.94) | data formatting | bytes 3145728
  276.5 42.9 %all_to_all.36 = bf16[32,2,12288]{2,1,0:T(2,128)(2,1)} all-to-all(bf16[32,2,12288]{2,1,0:T(2,128)(2,1)} %reshape.95), channel_id=1, replica_groups=mesh['star'=8,'row'=32] {'row'}, dimensions={0} | all-to-all | bytes 3145728 | tf_op jit(solution)/shard_map/all_to_all | solution.py:95
  319.5 14.3 %reshape.96 = bf16[1024,12,2,32]{3,2,1,0:T(2,128)(2,1)} reshape(bf16[32,2,12288]{2,1,0:T(2,128)(2,1)} %all_to_all.36) | data formatting | bytes 3145728
  333.7 9.5 %copy.106 = bf16[12,2,32,32,32]{2,3,4,1,0:T(8,128)(2,1)} copy(bf16[12,2,32,32,32]{2,1,0,4,3:T(2,128)(2,1)} %bitcast.91) | data formatting | bytes 3145728 | tf_op jit(solution)/shard_map/all_to_all | solution.py:95
  343.2 9.8 %all_to_all.33 = bf16[12,2,1024,32]{2,3,1,0:T(8,128)(2,1)} reshape(bf16[12,2,32,32,32]{3,2,4,1,0:T(8,128)(2,1)} %bitcast.92) | data formatting | bytes 3145728 | tf_op jit(solution)/shard_map/all_to_all | solution.py:95
  353.0 18.3 %fusion.22 = f32[12,2,32,1024]{3,2,1,0:T(8,128)S(1)} fusion(bf16[12,2,1024,32]{2,3,1,0:T(8,128)(2,1)} %all_to_all.33), kind=kOutput, calls=%fused_computation.33 | convolution fusion | flops 1627389952 | bytes 4718592 | tf_op jit(solution)/shard_map/savr,vc->sarc/dot_general | solution.py:97
  371.3 17.0 %fusion.30 = f32[12,2,32,1024]{3,2,1,0:T(8,128)S(1)} fusion(bf16[12,2,1024,32]{2,3,1,0:T(8,128)(2,1)S(1)} %copy-done.4), kind=kOutput, calls=%fused_computation.37 | convolution fusion | flops 1626341376 | bytes 4718592 | tf_op jit(solution)/shard_map/savr,vc->sarc/dot_general | solution.py:96
  389.4 11.4 %fusion.19 = bf16[12,32,1024]{2,0,1:T(8,128)(2,1)S(1)} fusion(f32[12,1,32,1024]{3,2,1,0:T(8,128)S(1)} %get-tuple-element.24, f32[12,1,32,1024]{3,2,1,0:T(8,128)S(1)} %get-tuple-element.19, f32[12,1,32,1024]{3,2,1,0:T(8,128)S(1)} %get-tuple-element.25, f32[12,1,32,1024]{3,2,1,0:T(8,128)S(1)} %get-tuple-element.18, f32[12,32,1024]{2,0,1:T(8,128)S(1)} %fusion.3, ...), kind=kLoop, calls=%fused_computation.29 | loop fusion | flops 3538944 | bytes 8781872 | tf_op jit(solution)/shard_map/convert_element_type | solution.py:102
  413.6 78.1 %psum.7 = f32[64,64]{1,0:T(8,128)} all-reduce(f32[64,64]{1,0:T(8,128)S(1)} %fusion.57), channel_id=1, replica_groups=mesh['star'=8,'row'=32] {'star','row'}, use_global_device_ids=true, to_apply=%region_4.5 | all-reduce | flops 4096 | bytes 32768 | tf_op jit(solution)/shard_map/psum | solution.py:114
  (44 shorter events, 33.2 us)
Async XLA Ops:
  7.2 1.8 copy-start
  91.3 12.3 %copy-start.6 = (s32[8]{0:T(128)S(1)}, s32[8]{0:T(128)}, u32[]{:S(2)}) copy-start(s32[8]{0:T(128)} %param.8) | copy-start | bytes 100
  91.3 12.4 %copy-start.5 = (bf16[12,32,1024]{2,1,0:T(8,128)(2,1)S(1)}, bf16[12,32,1024]{2,1,0:T(8,128)(2,1)}, u32[]{:S(2)}) copy-start(bf16[12,32,1024]{2,1,0:T(8,128)(2,1)} %param.11) | copy-start | bytes 2359300
  91.3 50.2 %all-to-all-start = ((bf16[32,2,12288]{2,1,0:T(2,128)(2,1)}), bf16[32,2,12288]{2,1,0:T(2,128)(2,1)}, u32[]{:S(2)}, u32[]{:S(2)}) async-start(bf16[32,2,12288]{2,1,0:T(2,128)(2,1)} %reshape.93), calls=%async_computation | async-start | bytes 3145728 | tf_op jit(solution)/shard_map/all_to_all | solution.py:75
  103.6 388.1 %reduce-scatter.2.cloned.1.call-start = ((), (), s32[]{:S(2)}) async-start(), calls=%async_computation.3 | async-start | bytes 9437184 | tf_op jit(solution)/shard_map/reduce_scatter | solution.py:116
  175.0 18.3 %copy-start.3 = (bf16[12,2,1024,32]{2,3,1,0:T(8,128)(2,1)S(1)}, bf16[12,2,1024,32]{2,3,1,0:T(8,128)(2,1)}, u32[]{:S(2)}) copy-start(bf16[12,2,1024,32]{2,3,1,0:T(8,128)(2,1)} %all_to_all.29) | copy-start | bytes 4718596
  210.7 1.4 copy-start.2
  353.0 18.3 %copy-start.4 = (bf16[12,2,1024,32]{2,3,1,0:T(8,128)(2,1)S(1)}, bf16[12,2,1024,32]{2,3,1,0:T(8,128)(2,1)}, u32[]{:S(2)}) copy-start(bf16[12,2,1024,32]{2,3,1,0:T(8,128)(2,1)} %all_to_all.33) | copy-start | bytes 4718596
  406.5 88.0 %copy-start.1 = (bf16[64,64]{1,0:T(8,128)(2,1)S(1)}, bf16[64,64]{1,0:T(8,128)(2,1)}, u32[]{:S(2)}) copy-start(bf16[64,64]{1,0:T(8,128)(2,1)} %param.7) | copy-start | bytes 24580
Sparse Core Ops, SparseCore 0:
  406.6 54.6 reduce-scatter.1
where the time goes:
time: 509 us; the launch traced here: 502 us
  matrix products  158 us (31%)
  local copies, waits for them, and re-layouts  132 us (26%)
  blocking collectives  121 us (24%)
  waiting for transfers between devices  36.3 us (7%)
  other arithmetic  27.5 us (5%)
  between operations  14.7 us (3%)
  starting transfers between devices  12.3 us (2%)
    psum x1, blocking collectives, per_device(): coef_grad = lax.psum(coef_part, ('star', 'row'))  78.1 us
    unnamed x21, local copies, waits for them, and re-layouts  60.5 us
    all_to_all x1, blocking collectives, per_device(): lax.all_to_all(spectrum_grad, 'row', split_axis=3, concat_axis=2, tiled=T...  42.9 us
    all_to_all x1, waiting for transfers between devices, per_device(): lax.all_to_all(column_field, 'row', split_axis=3, concat_axis=2, tiled=True)  36.3 us
    all_to_all x2, local copies, waits for them, and re-layouts, per_device(): lax.all_to_all(column_field, 'row', split_axis=3, concat_axis=2, tiled=True)  19.3 us
    all_to_all x2, local copies, waits for them, and re-layouts, per_device(): lax.all_to_all(spectrum_grad, 'row', split_axis=3, concat_axis=2, tiled=T...  19.3 us
    dot_general x1, matrix products, per_device(): jnp.einsum('savr,vc->sarc', pieces, sin_table, preferred_element_type=jnp...  18.3 us
    dot_general x1, matrix products, per_device(): jnp.einsum('sarv,ru->savu', pieces, sin_table, preferred_element_type=jnp...  18.3 us
  transfers between devices with their start and end apart: 2, of which 1 were waited for; matrix products, arithmetic and copies ran while one was open for 2% of the time, Pallas kernels for 0%

commit v1 on v0

--- a/solution.py
+++ b/solution.py
@@ -111,7 +111,8 @@
         (((0,), (0,)), ((), ())),
         precision=lax.Precision.HIGHEST,
     )
-    coef_grad = lax.psum(coef_part, ("star", "row"))
+    shards = lax.all_gather(coef_part, ("star", "row"), axis=0, tiled=False)
+    coef_grad = shards.sum(axis=0)
     share = map_count // groups
     map_grad = lax.psum_scatter(
         lax.dot_general(

time: 509 us -> 552 us (1.084)
  waiting for transfers between devices: 36.3 us -> 152 us
  blocking collectives: 121 us -> 42.9 us
    all_gather x0 -> x1, waiting for transfers between devices: none -> 116 us  [per_device(): shards = lax.all_gather(coef_part, ('star', 'row'), axis=0, tiled=False)]
    psum x1 -> x0, blocking collectives: 78.1 us -> none  [per_device(): coef_grad = lax.psum(coef_part, ('star', 'row'))]
    unnamed x21 -> x23, local copies, waits for them, and re-layouts: 60.5 us -> 60.5 us
  transfers between devices with their start and end apart: 2 -> 3, of which waited for: 1 -> 2; matrix products, arithmetic and copies ran while one was open for 2% -> 2% of each run, Pallas kernels for 0% -> 0%
where the time goes in v1:
time: 552 us; the launch traced here: 544 us
  matrix products  156 us (28%)
  waiting for transfers between devices  152 us (28%)
  local copies, waits for them, and re-layouts  132 us (24%)
  blocking collectives  42.9 us (8%)
  other arithmetic  32.1 us (6%)
  between operations  16.2 us (3%)
  starting transfers between devices  12.4 us (2%)
    all_gather x1, waiting for transfers between devices, per_device(): shards = lax.all_gather(coef_part, ('star', 'row'), axis=0, tiled=False)  116 us
    unnamed x23, local copies, waits for them, and re-layouts  60.5 us
    all_to_all x1, blocking collectives, per_device(): lax.all_to_all(spectrum_grad, 'row', split_axis=3, concat_axis=2, tiled=T...  42.9 us
    all_to_all x1, waiting for transfers between devices, per_device(): lax.all_to_all(column_field, 'row', split_axis=3, concat_axis=2, tiled=True)  36.3 us
    all_to_all x2, local copies, waits for them, and re-layouts, per_device(): lax.all_to_all(column_field, 'row', split_axis=3, concat_axis=2, tiled=True)  19.2 us
    all_to_all x2, local copies, waits for them, and re-layouts, per_device(): lax.all_to_all(spectrum_grad, 'row', split_axis=3, concat_axis=2, tiled=T...  19.2 us
    dot_general x1, matrix products, per_device(): jnp.einsum('savr,vc->sarc', pieces, sin_table, preferred_element_type=jnp...  18.3 us
    dot_general x1, matrix products, per_device(): jnp.einsum('sarv,ru->savu', pieces, sin_table, preferred_element_type=jnp...  18.3 us
  transfers between devices with their start and end apart: 3, of which 2 were waited for; matrix products, arithmetic and copies ran while one was open for 2% of the time, Pallas kernels for 0%

profile of v1, /device:TPU:1, one launch (start us, length us, event | category | flops | bytes accessed | tf_op | source)
XLA Modules:
  0.0 544.1 jit_solution(18122331977936464397)
XLA Ops:
  16.8 8.4 %fusion.54 = (bf16[12,1,32,1024]{3,0,2,1:T(8,128)(2,1)S(1)}, bf16[12,1,32,1024]{3,0,2,1:T(8,128)(2,1)S(1)}) fusion(f32[12,32,1024]{2,0,1:T(8,128)S(1)} %fusion.3, f32[32,1024]{1,0:T(8,128)S(1)} %fusion.56, f32[12]{0:T(128)S(1)} %add_divide_fusion), kind=kLoop, calls=%fused_computation.67 | loop fusion | flops 1966080 | bytes 3276848 | tf_op jit(solution)/shard_map/stack | solution.py:63
  25.5 17.9 %fusion.28 = f32[12,2,32,1024]{3,2,1,0:T(8,128)S(1)} fusion(bf16[12,2,32,1024]{3,0,2,1:T(8,128)(2,1)S(1)} %pad_maximum_fusion), kind=kOutput, calls=%fused_computation.36 | convolution fusion | flops 1627389952 | bytes 4718592 | tf_op jit(solution)/shard_map/sarc,cv->sarv/dot_general | solution.py:69
  43.4 17.3 %fusion.36 = f32[12,2,32,1024]{3,2,1,0:T(8,128)S(1)} fusion(bf16[12,2,32,1024]{3,0,2,1:T(8,128)(2,1)S(1)} %pad_maximum_fusion), kind=kOutput, calls=%fused_computation.40 | convolution fusion | flops 1626341376 | bytes 4718592 | tf_op jit(solution)/shard_map/sarc,cv->sarv/dot_general | solution.py:66
  63.2 15.0 %copy.45 = bf16[12,2,32,1024]{2,1,0,3:T(2,128)(2,1)} copy(bf16[12,2,32,1024]{3,2,1,0:T(8,128)(2,1)} %pad_maximum_fusion.1) | data formatting | bytes 3145728 | tf_op jit(solution)/shard_map/stack | solution.py:72
  78.3 13.8 %reshape.94 = bf16[32,2,12288]{2,1,0:T(2,128)(2,1)} reshape(bf16[1024,12,2,32]{3,2,1,0:T(2,128)(2,1)} %bitcast.94) | data formatting | bytes 3145728
  92.1 12.3 %all-to-all-start = ((bf16[32,2,12288]{2,1,0:T(2,128)(2,1)}), bf16[32,2,12288]{2,1,0:T(2,128)(2,1)}, u32[]{:S(2)}, u32[]{:S(2)}) async-start(bf16[32,2,12288]{2,1,0:T(2,128)(2,1)} %reshape.94), calls=%async_computation | async-start | bytes 3145728 | tf_op jit(solution)/shard_map/all_to_all | solution.py:75
  106.0 36.3 %all-to-all-done = bf16[32,2,12288]{2,1,0:T(2,128)(2,1)} async-done(((bf16[32,2,12288]{2,1,0:T(2,128)(2,1)}), bf16[32,2,12288]{2,1,0:T(2,128)(2,1)}, u32[]{:S(2)}, u32[]{:S(2)}) %all-to-all-start) | async-done | bytes 1572896 | tf_op jit(solution)/shard_map/all_to_all | solution.py:75
  142.3 14.3 %reshape.95 = bf16[1024,12,2,32]{3,2,1,0:T(2,128)(2,1)} reshape(bf16[32,2,12288]{2,1,0:T(2,128)(2,1)} %all-to-all-done) | data formatting | bytes 3145728
  156.5 9.5 %copy.107 = bf16[12,2,32,32,32]{2,3,4,1,0:T(8,128)(2,1)} copy(bf16[12,2,32,32,32]{2,1,0,4,3:T(2,128)(2,1)} %bitcast.90) | data formatting | bytes 3145728 | tf_op jit(solution)/shard_map/all_to_all | solution.py:75
  166.0 9.8 %all_to_all.29 = bf16[12,2,1024,32]{2,3,1,0:T(8,128)(2,1)} reshape(bf16[12,2,32,32,32]{3,2,4,1,0:T(8,128)(2,1)} %bitcast.91) | data formatting | bytes 3145728 | tf_op jit(solution)/shard_map/all_to_all | solution.py:75
  175.8 18.3 %fusion.26 = f32[12,2,32,1024]{3,2,1,0:T(8,128)S(1)} fusion(bf16[12,2,1024,32]{2,3,1,0:T(8,128)(2,1)} %all_to_all.29), kind=kOutput, calls=%fused_computation.35 | convolution fusion | flops 1627389952 | bytes 4718592 | tf_op jit(solution)/shard_map/sarv,ru->savu/dot_general | solution.py:77
  194.1 17.4 %fusion.34 = f32[12,2,32,1024]{3,2,1,0:T(8,128)S(1)} fusion(bf16[12,2,1024,32]{2,3,1,0:T(8,128)(2,1)S(1)} %copy-done.4), kind=kOutput, calls=%fused_computation.39 | convolution fusion | flops 1626341376 | bytes 4718592 | tf_op jit(solution)/shard_map/sarv,ru->savu/dot_general | solution.py:76
  212.9 16.4 %fusion.32 = f32[12,2,32,1024]{3,2,1,0:T(8,128)S(1)} fusion(f32[12,1,32,1024]{3,2,1,0:T(8,128)S(1)} %get-tuple-element.15, f32[12,1,32,1024]{3,2,1,0:T(8,128)S(1)} %get-tuple-element.14, f32[12,32,1024]{2,1,0:T(8,128)S(1)} %copy-done.3), kind=kOutput, calls=%fused_computation.38 | convolution fusion | flops 1628700672 | bytes 7864320 | tf_op jit(solution)/shard_map/savu,ur->savr/dot_general | solution.py:85
  229.3 16.7 %fusion.24 = f32[12,2,32,1024]{3,2,1,0:T(8,128)S(1)} fusion(f32[12,1,32,1024]{3,2,1,0:T(8,128)S(1)} %get-tuple-element.15, f32[12,1,32,1024]{3,2,1,0:T(8,128)S(1)} %get-tuple-element.14, f32[12,32,1024]{2,1,0:T(8,128)S(1)} %copy-done.3), kind=kOutput, calls=%fused_computation.34 | convolution fusion | flops 1629749248 | bytes 7864320 | tf_op jit(solution)/shard_map/savu,ur->savr/dot_general | solution.py:88
  248.0 15.0 %copy.47 = bf16[12,2,32,1024]{2,1,0,3:T(2,128)(2,1)} copy(bf16[12,2,32,1024]{3,2,1,0:T(8,128)(2,1)} %pad_maximum_fusion.2) | data formatting | bytes 3145728 | tf_op jit(solution)/shard_map/stack | solution.py:91
  263.1 14.2 %reshape.96 = bf16[32,2,12288]{2,1,0:T(2,128)(2,1)} reshape(bf16[1024,12,2,32]{3,2,1,0:T(2,128)(2,1)} %bitcast.95) | data formatting | bytes 3145728
  277.3 42.9 %all_to_all.36 = bf16[32,2,12288]{2,1,0:T(2,128)(2,1)} all-to-all(bf16[32,2,12288]{2,1,0:T(2,128)(2,1)} %reshape.96), channel_id=1, replica_groups=mesh['star'=8,'row'=32] {'row'}, dimensions={0} | all-to-all | bytes 3145728 | tf_op jit(solution)/shard_map/all_to_all | solution.py:95
  320.2 14.3 %reshape.97 = bf16[1024,12,2,32]{3,2,1,0:T(2,128)(2,1)} reshape(bf16[32,2,12288]{2,1,0:T(2,128)(2,1)} %all_to_all.36) | data formatting | bytes 3145728
  334.5 9.5 %copy.106 = bf16[12,2,32,32,32]{2,3,4,1,0:T(8,128)(2,1)} copy(bf16[12,2,32,32,32]{2,1,0,4,3:T(2,128)(2,1)} %bitcast.92) | data formatting | bytes 3145728 | tf_op jit(solution)/shard_map/all_to_all | solution.py:95
  343.9 9.8 %all_to_all.33 = bf16[12,2,1024,32]{2,3,1,0:T(8,128)(2,1)} reshape(bf16[12,2,32,32,32]{3,2,4,1,0:T(8,128)(2,1)} %bitcast.93) | data formatting | bytes 3145728 | tf_op jit(solution)/shard_map/all_to_all | solution.py:95
  353.7 18.3 %fusion.22 = f32[12,2,32,1024]{3,2,1,0:T(8,128)S(1)} fusion(bf16[12,2,1024,32]{2,3,1,0:T(8,128)(2,1)} %all_to_all.33), kind=kOutput, calls=%fused_computation.33 | convolution fusion | flops 1627389952 | bytes 4718592 | tf_op jit(solution)/shard_map/savr,vc->sarc/dot_general | solution.py:97
  372.0 17.0 %fusion.30 = f32[12,2,32,1024]{3,2,1,0:T(8,128)S(1)} fusion(bf16[12,2,1024,32]{2,3,1,0:T(8,128)(2,1)S(1)} %copy-done.5), kind=kOutput, calls=%fused_computation.37 | convolution fusion | flops 1626341376 | bytes 4718592 | tf_op jit(solution)/shard_map/savr,vc->sarc/dot_general | solution.py:96
  390.1 11.4 %fusion.19 = bf16[12,32,1024]{2,0,1:T(8,128)(2,1)S(1)} fusion(f32[12,1,32,1024]{3,2,1,0:T(8,128)S(1)} %get-tuple-element.24, f32[12,1,32,1024]{3,2,1,0:T(8,128)S(1)} %get-tuple-element.19, f32[12,1,32,1024]{3,2,1,0:T(8,128)S(1)} %get-tuple-element.25, f32[12,1,32,1024]{3,2,1,0:T(8,128)S(1)} %get-tuple-element.18, f32[12,32,1024]{2,0,1:T(8,128)S(1)} %fusion.3, ...), kind=kLoop, calls=%fused_computation.29 | loop fusion | flops 3538944 | bytes 8781872 | tf_op jit(solution)/shard_map/convert_element_type | solution.py:102
  412.8 116.0 %all-gather.3.cloned.1.call-done = f32[16384,64]{1,0:T(8,128)} async-done(((f32[64,64]{1,0:T(8,128)}), f32[16384,64]{1,0:T(8,128)}) %all-gather.3.cloned.1.call-update) | async-done | bytes 4194320 | tf_op jit(solution)/shard_map/all_gather | solution.py:114
  (49 shorter events, 36.3 us)
Async XLA Ops:
  8.0 1.8 copy-start
  92.1 12.3 %copy-start.7 = (s32[8]{0:T(128)S(1)}, s32[8]{0:T(128)}, u32[]{:S(2)}) copy-start(s32[8]{0:T(128)} %param.8) | copy-start | bytes 100
  92.1 12.4 %copy-start.6 = (bf16[12,32,1024]{2,1,0:T(8,128)(2,1)S(1)}, bf16[12,32,1024]{2,1,0:T(8,128)(2,1)}, u32[]{:S(2)}) copy-start(bf16[12,32,1024]{2,1,0:T(8,128)(2,1)} %param.11) | copy-start | bytes 2359300
  92.1 50.2 %all-to-all-start = ((bf16[32,2,12288]{2,1,0:T(2,128)(2,1)}), bf16[32,2,12288]{2,1,0:T(2,128)(2,1)}, u32[]{:S(2)}, u32[]{:S(2)}) async-start(bf16[32,2,12288]{2,1,0:T(2,128)(2,1)} %reshape.94), calls=%async_computation | async-start | bytes 3145728 | tf_op jit(solution)/shard_map/all_to_all | solution.py:75
  104.4 424.3 %all-gather.3.cloned.1.call-start = ((), (), s32[]{:S(2)}) async-start(), calls=%async_computation.4 | async-start | bytes 8421376 | tf_op jit(solution)/shard_map/all_gather | solution.py:114
  175.8 18.3 %copy-start.4 = (bf16[12,2,1024,32]{2,3,1,0:T(8,128)(2,1)S(1)}, bf16[12,2,1024,32]{2,3,1,0:T(8,128)(2,1)}, u32[]{:S(2)}) copy-start(bf16[12,2,1024,32]{2,3,1,0:T(8,128)(2,1)} %all_to_all.29) | copy-start | bytes 4718596
  211.5 1.4 copy-start.3
  353.7 18.3 %copy-start.5 = (bf16[12,2,1024,32]{2,3,1,0:T(8,128)(2,1)S(1)}, bf16[12,2,1024,32]{2,3,1,0:T(8,128)(2,1)}, u32[]{:S(2)}) copy-start(bf16[12,2,1024,32]{2,3,1,0:T(8,128)(2,1)} %all_to_all.33) | copy-start | bytes 4718596
  390.1 11.4 %copy-start.2 = (bf16[64,32,1024]{2,1,0:T(8,128)(2,1)S(1)}, bf16[64,32,1024]{2,1,0:T(8,128)(2,1)}, u32[]{:S(2)}) copy-start(bf16[64,32,1024]{2,1,0:T(8,128)(2,1)} %param.6) | copy-start | bytes 12582916
  407.0 126.3 %reduce-scatter.2.cloned.1.call-start = ((), (), s32[]{:S(2)}) async-start(), calls=%async_computation.3 | async-start | bytes 9437184 | tf_op jit(solution)/shard_map/reduce_scatter | solution.py:117
  528.7 7.4 %copy-start.1 = (bf16[64,64]{1,0:T(8,128)(2,1)S(1)}, bf16[64,64]{1,0:T(8,128)(2,1)}, u32[]{:S(2)}) copy-start(bf16[64,64]{1,0:T(8,128)(2,1)} %param.7) | copy-start | bytes 24580
Sparse Core Ops, SparseCore 0:
  407.2 121.5 all-gather.2
Sparse Core Ops, SparseCore 1:
  412.9 55.5 reduce-scatter.1
